TPU v7x, 32 devices: a whole 2x2x4 slice. The times are simulated.
32 devices in a mesh: dp: 4 (over y, core), cells: 8 (over z, x).
Axes of the slice: x: 2, y: 2, z: 4, core: 2. Of those that a mesh axis runs over, the one named last changes fastest.
Arguments:
- sensitivity: float32 [8192, 12288], P('dp', 'cells'), may hold values from -0.0546875 to 0.0546875
- observed: float32 [8192, 256], P('dp'), may hold values from -6 to 6
- models: float32 [12288, 256], P('cells'), may hold values from -6 to 6
- neighbour_map: int32 [4, 768], replicated, may hold values from 0 to 767, as said below
- edge_mask: int32 [12288], P('cells'), may hold values 0 or 1
Outputs:
- updated: float32 [12288, 256], P('cells')
Inputs may be any that keep to these rules, and one draw needn't show every extreme that they name: `neighbour_map`: each row k maps every cell of a periodic 32 by 24 plane grid, numbered in a drawn order, to its neighbour in one of the four grid directions; every row is a permutation.
All inputs are finite; a program needn't handle non-finite values. No bound on the sum of `edge_mask` on one device may be relied on, other than what follows from the above.
Results may differ from a plain program's by a relative error of at most 0.0001.
Values sent between devices are 32-bit elements; how exact they have to be, the bound alone decides.
A program may use at most 128 MiB of HBM per device.

v0:
```python
import jax
import jax.numpy as jnp
from jax import lax
from jax.sharding import PartitionSpec as P

ITERS = 2


def with_halo(cells, sides, width):
    for axis, dim in sides:
        count = lax.axis_size(axis)
        ends = count - 1
        head = lax.slice_in_dim(cells, 0, width, axis=dim)
        tail = lax.slice_in_dim(cells, cells.shape[dim] - width, cells.shape[dim], axis=dim)
        cells = jnp.concatenate(
            [
                lax.ppermute(tail, axis, [(i, (i + 1) % count) for i in range(ends)]),
                cells,
                lax.ppermute(head, axis, [((i + 1) % count, i) for i in range(ends)]),
            ],
            axis=dim,
        )
    return cells


def reweight(misfit):
    return misfit / jnp.maximum(jnp.abs(misfit), 1.0)


def smooth_local(current, neighbour_map, edge_mask):
    plane_cells = neighbour_map.shape[1]
    count = current.shape[0] // plane_cells
    planes = current.reshape(count, plane_cells, current.shape[1])
    padded = with_halo(planes, (("cells", 0),), 1)
    total = jnp.zeros_like(planes)
    for other in (padded[:-2], padded[2:]):
        diff = other - planes
        total = total + diff / jnp.sqrt(1.0 + diff * diff)
    for k in range(4):
        other = jnp.take(planes, neighbour_map[k], axis=1)
        diff = other - planes
        total = total + diff / jnp.sqrt(1.0 + diff * diff)
    scale = 1.0 - 0.75 * edge_mask.astype(jnp.float32).reshape(count, plane_cells, 1)
    return (total * scale).reshape(current.shape)


def local(sensitivity, observed, models, neighbour_map, edge_mask):
    current = models
    for step in range(ITERS):
        predicted = lax.psum(
            jnp.dot(
                sensitivity,
                current,
                precision=lax.Precision.HIGHEST,
                preferred_element_type=jnp.float32,
            ),
            "cells",
        )
        weighted = reweight(predicted - observed)
        smooth = smooth_local(current, neighbour_map, edge_mask)
        partial_grad = lax.dot_general(
            sensitivity,
            weighted,
            (((0,), (0,)), ((), ())),
            precision=lax.Precision.HIGHEST,
            preferred_element_type=jnp.float32,
        )
        gradient = lax.psum(partial_grad, "dp")
        current = current - 1.0 * gradient + 0.05 * smooth
    return current


def solution(mesh):
    return jax.shard_map(
        local,
        mesh=mesh,
        in_specs=(P("dp", "cells"), P("dp", None), P("cells", None), P(), P("cells")),
        out_specs=P("cells", None),
        check_vma=False,
    )
```

profile of v0, /device:TPU:0, one launch (start us, length us, event | category | flops | bytes accessed | tf_op | source)
XLA Modules:
  0.0 418.7 jit_solution(4675436302633939359)
XLA Ops:
  6.5 13.9 %fusion.16 = f32[2048,256]{1,0:T(8,128)} fusion(f32[2048,1536]{1,0:T(8,128)} %param.7, f32[1536,256]{1,0:T(8,128)} %param.9), kind=kOutput, calls=%fused_computation.72 | convolution fusion | flops 9663676416 | bytes 16252928 | tf_op jit(solution)/shard_map/dot_general | solution.py:51
  20.6 1.3 copy-done
  21.9 1.3 slice_bitcast_fusion.3
  23.1 5.7 %collective-permute-start = (f32[1,768,256]{2,1,0:T(8,128)}, f32[1,768,256]{2,1,0:T(8,128)}, u32[]{:S(2)}, u32[]{:S(2)}) collective-permute-start(f32[1,768,256]{2,1,0:T(8,128)} %get-tuple-element.12), channel_id=1, source_target_pairs={{0,1},{1,2},{2,3},{3,4},{4,5},{5,6},{6,7},{8,9},{9,10},{10,11},{11... | collective-permute-start | bytes 2359304 | tf_op jit(solution)/shard_map/ppermute | solution.py:17
  28.9 1.3 collective-permute-start.1
  30.2 1.2 copy.73
  31.5 4.0 gather_fusion.3
  35.5 4.0 gather_fusion.2
  39.6 4.0 gather_fusion.1
  43.6 4.1 gather_fusion
  47.7 96.1 %all-reduce.5.cloned.1.call-done = f32[2048,256]{1,0:T(8,128)} async-done(((f32[2048,256]{1,0:T(8,128)}), f32[2048,256]{1,0:T(8,128)}) %all-reduce.5.cloned.1.call-update) | async-done | bytes 2097168 | tf_op jit(solution)/shard_map/psum | solution.py:50
  143.8 25.0 %convolution_bitcast_fusion.2 = f32[1536,256]{1,0:T(8,128)} fusion(f32[2048,1536]{1,0:T(8,128)} %param.7, f32[2048,256]{1,0:T(8,128)} %all-reduce.5.cloned.1.call-done, f32[2048,256]{1,0:T(8,128)} %param.8), kind=kOutput, calls=%fused_computation.10 | convolution fusion | flops 9665773568 | bytes 18350080 | tf_op jit(solution)/shard_map/dot_general | solution.py:61
  168.8 0.0 all-reduce.9.cloned.1.call-start
  168.9 1.3 copy-done.1
  170.2 6.2 %multiply_multiply_fusion.1 = f32[2,768,256]{2,1,0:T(8,128)} fusion(f32[2,768,256]{2,1,0:T(8,128)S(1)} %bitcast.61, f32[768,2,256]{2,1,0:T(2,128)S(1)} %copy-done.1, f32[768,2,256]{2,1,0:T(2,128)} %gather_fusion.2, f32[768,2,256]{2,1,0:T(2,128)} %gather_fusion.1, f32[768,2,256]{2,1,0:T(2,128)} %gather_fusion, f32[1,768,256]{2,1,0:T(8,128)} %collective-permute-done.1, ...), kind=kLoop, calls=%fused_computation.46 | loop fusion | flops 14548992 | bytes 11019264 | tf_op jit(solution)/shard_map/mul | solution.py:69
  176.4 34.7 %all-reduce.7.cloned.1.call-done = f32[1536,256]{1,0:T(8,128)} async-done(((f32[1536,256]{1,0:T(8,128)}), f32[1536,256]{1,0:T(8,128)}) %all-reduce.7.cloned.1.call-update) | async-done | bytes 1572880 | tf_op jit(solution)/shard_map/psum | solution.py:68
  211.1 2.2 bitcast_add_fusion.1
  213.3 13.5 %convolution_bitcast_fusion.1 = f32[2048,256]{1,0:T(8,128)} fusion(f32[1536,256]{1,0:T(8,128)S(1)} %bitcast_add_fusion.1, f32[2048,1536]{1,0:T(8,128)} %param.7), kind=kOutput, calls=%fused_computation.9 | convolution fusion | flops 9663676416 | bytes 16252928 | tf_op jit(solution)/shard_map/dot_general | solution.py:51
  226.9 1.2 copy.83
  228.1 4.0 gather_fusion.7
  232.1 4.0 gather_fusion.6
  236.1 4.0 gather_fusion.5
  240.2 4.1 gather_fusion.4
  244.2 1.3 slice_bitcast_fusion.1
  245.5 4.2 %collective-permute-start.2 = (f32[1,768,256]{2,1,0:T(8,128)}, f32[1,768,256]{2,1,0:T(8,128)}, u32[]{:S(2)}, u32[]{:S(2)}) collective-permute-start(f32[1,768,256]{2,1,0:T(8,128)} %get-tuple-element.10), channel_id=1, source_target_pairs={{0,1},{1,2},{2,3},{3,4},{4,5},{5,6},{6,7},{8,9},{9,10},{10,11},{11... | collective-permute-start | bytes 2359304 | tf_op jit(solution)/shard_map/ppermute | solution.py:17
  249.7 1.3 collective-permute-start.3
  251.0 90.5 %all-reduce.9.cloned.1.call-done = f32[2048,256]{1,0:T(8,128)} async-done(((f32[2048,256]{1,0:T(8,128)}), f32[2048,256]{1,0:T(8,128)}) %all-reduce.9.cloned.1.call-update) | async-done | bytes 2097168 | tf_op jit(solution)/shard_map/psum | solution.py:50
  341.5 24.8 %convolution_bitcast_fusion = f32[1536,256]{1,0:T(8,128)} fusion(f32[2048,1536]{1,0:T(8,128)} %param.7, f32[2048,256]{1,0:T(8,128)} %all-reduce.9.cloned.1.call-done, f32[2048,256]{1,0:T(8,128)} %param.8), kind=kOutput, calls=%fused_computation.8 | convolution fusion | flops 9665773568 | bytes 18350080 | tf_op jit(solution)/shard_map/dot_general | solution.py:61
  366.3 1.4 copy-done.2
  367.7 6.1 %multiply_multiply_fusion = f32[2,768,256]{2,1,0:T(8,128)} fusion(f32[2,768,256]{2,1,0:T(8,128)S(1)} %bitcast.59, f32[768,2,256]{2,1,0:T(2,128)S(1)} %copy-done.2, f32[768,2,256]{2,1,0:T(2,128)} %gather_fusion.6, f32[768,2,256]{2,1,0:T(2,128)} %gather_fusion.5, f32[768,2,256]{2,1,0:T(2,128)} %gather_fusion.4, f32[1,768,256]{2,1,0:T(8,128)} %collective-permute-done.3, ...), kind=kLoop, calls=%fused_computation.45 | loop fusion | flops 14548992 | bytes 11019264 | tf_op jit(solution)/shard_map/mul | solution.py:69
  373.8 34.8 %all-reduce.11.cloned.1.call-done = f32[1536,256]{1,0:T(8,128)} async-done(((f32[1536,256]{1,0:T(8,128)}), f32[1536,256]{1,0:T(8,128)}) %all-reduce.11.cloned.1.call-update) | async-done | bytes 1572880 | tf_op jit(solution)/shard_map/psum | solution.py:68
  408.6 3.3 bitcast_add_fusion
  (29 shorter events, 0.3 us)
Async XLA Ops:
  6.5 137.2 %all-reduce.5.cloned.1.call-start = ((), (), s32[]{:S(2)}) async-start(), calls=%async_computation | async-start | bytes 4194304 | tf_op jit(solution)/shard_map/psum | solution.py:50
  20.5 1.4 copy-start
  20.5 9.7 %copy-start.4 = (s32[1536]{0:T(1024)S(1)}, s32[1536]{0:T(1024)}, u32[]{:S(2)}) copy-start(s32[1536]{0:T(1024)} %param.11) | copy-start | bytes 18436
  20.5 190.6 %all-reduce.7.cloned.1.call-start = ((), (), s32[]{:S(2)}) async-start(), calls=%async_computation.1 | async-start | bytes 3145728 | tf_op jit(solution)/shard_map/psum | solution.py:68
  23.1 145.7 %collective-permute-start = (f32[1,768,256]{2,1,0:T(8,128)}, f32[1,768,256]{2,1,0:T(8,128)}, u32[]{:S(2)}, u32[]{:S(2)}) collective-permute-start(f32[1,768,256]{2,1,0:T(8,128)} %get-tuple-element.12), channel_id=1, source_target_pairs={{0,1},{1,2},{2,3},{3,4},{4,5},{5,6},{6,7},{8,9},{9,10},{10,11},{11... | collective-permute-start | bytes 2359304 | tf_op jit(solution)/shard_map/ppermute | solution.py:17
  28.9 140.0 %collective-permute-start.1 = (f32[1,768,256]{2,1,0:T(8,128)}, f32[1,768,256]{2,1,0:T(8,128)}, u32[]{:S(2)}, u32[]{:S(2)}) collective-permute-start(f32[1,768,256]{2,1,0:T(8,128)} %get-tuple-element.13), channel_id=1, source_target_pairs={{1,0},{2,1},{3,2},{4,3},{5,4},{6,5},{7,6},{9,8},{10,9},{11,10},{12... | collective-permute-start | bytes 2359304 | tf_op jit(solution)/shard_map/ppermute | solution.py:19
  30.2 1.2 copy-start.3
  168.8 1.4 copy-start.1
  168.8 172.7 %all-reduce.9.cloned.1.call-start = ((), (), s32[]{:S(2)}) async-start(), calls=%async_computation.2 | async-start | bytes 4194304 | tf_op jit(solution)/shard_map/psum | solution.py:50
  226.8 181.8 %all-reduce.11.cloned.1.call-start = ((), (), s32[]{:S(2)}) async-start(), calls=%async_computation.3 | async-start | bytes 3145728 | tf_op jit(solution)/shard_map/psum | solution.py:68
  245.5 120.8 %collective-permute-start.2 = (f32[1,768,256]{2,1,0:T(8,128)}, f32[1,768,256]{2,1,0:T(8,128)}, u32[]{:S(2)}, u32[]{:S(2)}) collective-permute-start(f32[1,768,256]{2,1,0:T(8,128)} %get-tuple-element.10), channel_id=1, source_target_pairs={{0,1},{1,2},{2,3},{3,4},{4,5},{5,6},{6,7},{8,9},{9,10},{10,11},{11... | collective-permute-start | bytes 2359304 | tf_op jit(solution)/shard_map/ppermute | solution.py:17
  249.7 116.6 %collective-permute-start.3 = (f32[1,768,256]{2,1,0:T(8,128)}, f32[1,768,256]{2,1,0:T(8,128)}, u32[]{:S(2)}, u32[]{:S(2)}) collective-permute-start(f32[1,768,256]{2,1,0:T(8,128)} %get-tuple-element.11), channel_id=1, source_target_pairs={{1,0},{2,1},{3,2},{4,3},{5,4},{6,5},{7,6},{9,8},{10,9},{11,10},{12... | collective-permute-start | bytes 2359304 | tf_op jit(solution)/shard_map/ppermute | solution.py:19
  366.3 1.4 copy-start.2
Sparse Core Ops, SparseCore 0:
  20.6 123.1 all-reduce.4
  168.9 42.1 all-reduce.6
  227.0 114.5 all-reduce.8
  366.4 42.1 all-reduce.10
where the time goes:
time: 426 us; the launch traced here: 419 us
  waiting for transfers between devices  256 us (60%)
  matrix products  77.2 us (18%)
  local copies, waits for them, and re-layouts  41.2 us (10%)
  other arithmetic  17.9 us (4%)
  between operations  13.5 us (3%)
  starting transfers between devices  12.7 us (3%)
    psum x2, waiting for transfers between devices, local(): lax.psum(jnp.dot(sensitivity, current, precision=lax.Precision.HIGHEST, p...  187 us
    psum x2, waiting for transfers between devices, local(): gradient = lax.psum(partial_grad, 'dp')  69.5 us
    dot_general x2, matrix products, local(): lax.dot_general(sensitivity, weighted, (((0,), (0,)), ((), ())), precisio...  49.8 us
    gather x8, local copies, waits for them, and re-layouts, smooth_local(): other = jnp.take(planes, neighbour_map[k], axis=1)  32.2 us
    dot_general x2, matrix products, local(): jnp.dot(sensitivity, current, precision=lax.Precision.HIGHEST, preferred_...  27.5 us
    mul x2, other arithmetic, local(): current = current - 1.0 * gradient + 0.05 * smooth  12.3 us
    ppermute x2, starting transfers between devices, with_halo(): lax.ppermute(tail, axis, [(i, (i + 1) % count) for i in range(ends)])  9.98 us
  transfers between devices with their start and end apart: 8, of which 4 were waited for; matrix products, arithmetic and copies ran while one was open for 24% of the time, Pallas kernels for 0%

commit v1 on v0

--- a/solution.py
+++ b/solution.py
@@ -47,15 +47,14 @@
 def local(sensitivity, observed, models, neighbour_map, edge_mask):
     current = models
     for step in range(ITERS):
-        predicted = lax.psum(
-            jnp.dot(
-                sensitivity,
-                current,
-                precision=lax.Precision.HIGHEST,
-                preferred_element_type=jnp.float32,
-            ),
-            "cells",
+        block = jnp.dot(
+            sensitivity,
+            current,
+            precision=lax.Precision.HIGHEST,
+            preferred_element_type=jnp.float32,
         )
+        parts = lax.all_gather(block, "cells", axis=0, tiled=False)
+        predicted = parts.sum(axis=0)
         weighted = reweight(predicted - observed)
         smooth = smooth_local(current, neighbour_map, edge_mask)
         partial_grad = lax.dot_general(

time: 426 us -> 720 us (1.69)
  waiting for transfers between devices: 256 us -> 503 us
  local copies, waits for them, and re-layouts: 41.2 us -> 61.7 us
  other arithmetic: 17.9 us -> 32.7 us
  matrix products: 77.2 us -> 87.4 us
    all_gather x0 -> x2, waiting for transfers between devices: none -> 435 us  [local(): parts = lax.all_gather(block, 'cells', axis=0, tiled=False)]
    psum x2 -> x0, waiting for transfers between devices: 187 us -> none  [local(): lax.psum(jnp.dot(sensitivity, current, precision=lax.Precision.HIGHEST, p...]
    unnamed x10 -> x11, local copies, waits for them, and re-layouts: 4.01 us -> 21.6 us
    reduce_sum x0 -> x2, other arithmetic: none -> 15.2 us  [local(): predicted = parts.sum(axis=0)]
    dot_general x2, matrix products: 27.5 us -> 38 us  [local(): jnp.dot(sensitivity, current, precision=lax.Precision.HIGHEST, preferred_...]
  transfers between devices with their start and end apart: 8 -> 8, of which waited for: 4 -> 4; matrix products, arithmetic and copies ran while one was open for 24% -> 19% of each run, Pallas kernels for 0% -> 0%
where the time goes in v1:
time: 720 us; the launch traced here: 712 us
  waiting for transfers between devices  503 us (70%)
  matrix products  87.4 us (12%)
  local copies, waits for them, and re-layouts  61.7 us (9%)
  other arithmetic  32.7 us (5%)
  between operations  13.5 us (2%)
  starting transfers between devices  13.2 us (2%)
    all_gather x2, waiting for transfers between devices, local(): parts = lax.all_gather(block, 'cells', axis=0, tiled=False)  435 us
    psum x2, waiting for transfers between devices, local(): gradient = lax.psum(partial_grad, 'dp')  67.6 us
    dot_general x2, matrix products, local(): lax.dot_general(sensitivity, weighted, (((0,), (0,)), ((), ())), precisio...  49.5 us
    dot_general x2, matrix products, local(): jnp.dot(sensitivity, current, precision=lax.Precision.HIGHEST, preferred_...  38 us
    gather x8, local copies, waits for them, and re-layouts, smooth_local(): other = jnp.take(planes, neighbour_map[k], axis=1)  32.1 us
    unnamed x11, local copies, waits for them, and re-layouts  21.6 us
    reduce_sum x2, other arithmetic, local(): predicted = parts.sum(axis=0)  15.2 us
  transfers between devices with their start and end apart: 8, of which 4 were waited for; matrix products, arithmetic and copies ran while one was open for 19% of the time, Pallas kernels for 0%

profile of v1, /device:TPU:0, one launch (start us, length us, event | category | flops | bytes accessed | tf_op | source)
XLA Modules:
  0.0 711.7 jit_solution(16524376959208173480)
XLA Ops:
  6.5 13.9 %fusion.16 = f32[2048,256]{1,0:T(8,128)} fusion(f32[2048,1536]{1,0:T(8,128)} %param.7, f32[1536,256]{1,0:T(8,128)} %param.9), kind=kOutput, calls=%fused_computation.73 | convolution fusion | flops 9663676416 | bytes 16252928 | tf_op jit(solution)/shard_map/dot_general | solution.py:50
  20.6 1.3 copy-done
  21.9 1.3 slice_bitcast_fusion.3
  23.2 5.8 collective-permute-start
  29.0 1.3 collective-permute-start.1
  31.6 4.0 gather_fusion.2
  35.6 4.0 gather_fusion
  39.7 4.0 gather_fusion.1
  43.7 4.0 gather_fusion.3
  47.7 216.2 %all-gather.5.cloned.1.call-done = f32[16384,256]{1,0:T(8,128)} async-done(((f32[2048,256]{1,0:T(8,128)}), f32[16384,256]{1,0:T(8,128)}) %all-gather.5.cloned.1.call-update) | async-done | bytes 16777232 | tf_op jit(solution)/shard_map/all_gather | solution.py:56
  263.9 8.5 %reduce_sum.18 = f32[2048,256]{1,0:T(8,128)} reduce(f32[8,2048,256]{2,1,0:T(8,128)} %bitcast.68, f32[]{:T(128)} %constant.0.clone.1), dimensions={0}, to_apply=%region_0.0 | reduce | flops 3670016 | bytes 18874372 | tf_op jit(solution)/shard_map/reduce_sum | solution.py:57
  272.4 24.7 %convolution_bitcast_fusion.2 = f32[1536,256]{1,0:T(8,128)} fusion(f32[2048,1536]{1,0:T(8,128)} %param.7, f32[2048,256]{1,0:T(8,128)} %reduce_sum.18, f32[2048,256]{1,0:T(8,128)} %param.8), kind=kOutput, calls=%fused_computation.11 | convolution fusion | flops 9665773568 | bytes 18350080 | tf_op jit(solution)/shard_map/dot_general | solution.py:60
  297.2 1.3 copy-done.1
  298.5 6.0 multiply_multiply_fusion.1
  304.6 33.8 %all-reduce.3.cloned.1.call-done = f32[1536,256]{1,0:T(8,128)} async-done(((f32[1536,256]{1,0:T(8,128)}), f32[1536,256]{1,0:T(8,128)}) %all-reduce.3.cloned.1.call-update) | async-done | bytes 1572880 | tf_op jit(solution)/shard_map/psum | solution.py:67
  338.3 2.2 bitcast_add_fusion.1
  340.5 24.0 %convolution_bitcast_fusion.1 = f32[2048,256]{0,1:T(8,128)} fusion(f32[1536,256]{1,0:T(8,128)S(1)} %bitcast_add_fusion.1, f32[2048,1536]{1,0:T(8,128)} %param.7), kind=kOutput, calls=%fused_computation.10 | convolution fusion | flops 9663676416 | bytes 16252928 | tf_op jit(solution)/shard_map/dot_general | solution.py:50
  366.2 4.0 gather_fusion.4
  370.3 4.0 gather_fusion.5
  374.3 4.0 gather_fusion.6
  378.3 4.0 gather_fusion.7
  382.3 1.3 slice_bitcast_fusion.1
  383.6 4.3 collective-permute-start.2
  389.2 219.3 %all-gather.7.cloned.1.call-done = f32[16384,256]{0,1:T(8,128)} async-done(((f32[2048,256]{0,1:T(8,128)}), f32[16384,256]{0,1:T(8,128)}) %all-gather.7.cloned.1.call-update) | async-done | bytes 16777232 | tf_op jit(solution)/shard_map/all_gather | solution.py:56
  608.5 17.6 %copy.155 = f32[32,8,8,2048]{3,2,1,0:T(8,128)S(1)} copy(f32[32,8,8,2048]{3,1,2,0:T(8,128)} %bitcast.69) | data formatting | bytes 33554432
  626.1 6.7 bitcast_reduce_fusion
  632.8 2.9 copy.143
  635.7 24.7 %convolution_bitcast_fusion = f32[1536,256]{1,0:T(8,128)} fusion(f32[2048,1536]{1,0:T(8,128)} %param.7, f32[2048,256]{1,0:T(8,128)} %copy.143, f32[2048,256]{1,0:T(8,128)} %param.8), kind=kOutput, calls=%fused_computation.9 | convolution fusion | flops 9665773568 | bytes 18350080 | tf_op jit(solution)/shard_map/dot_general | solution.py:60
  660.5 1.4 copy-done.2
  661.8 6.0 multiply_multiply_fusion
  667.8 33.8 %all-reduce.5.cloned.1.call-done = f32[1536,256]{1,0:T(8,128)} async-done(((f32[1536,256]{1,0:T(8,128)}), f32[1536,256]{1,0:T(8,128)}) %all-reduce.5.cloned.1.call-update) | async-done | bytes 1572880 | tf_op jit(solution)/shard_map/psum | solution.py:67
  701.6 3.3 bitcast_add_fusion
  (33 shorter events, 4.4 us)
Async XLA Ops:
  6.5 257.4 %all-gather.5.cloned.1.call-start = ((), (), s32[]{:S(2)}) async-start(), calls=%async_computation.2 | async-start | bytes 18874368 | tf_op jit(solution)/shard_map/all_gather | solution.py:56
  20.5 1.4 copy-start
  20.5 317.8 %all-reduce.3.cloned.1.call-start = ((), (), s32[]{:S(2)}) async-start(), calls=%async_computation | async-start | bytes 3145728 | tf_op jit(solution)/shard_map/psum | solution.py:67
  23.2 274.0 %collective-permute-start = (f32[1,768,256]{2,1,0:T(8,128)}, f32[1,768,256]{2,1,0:T(8,128)}, u32[]{:S(2)}, u32[]{:S(2)}) collective-permute-start(f32[1,768,256]{2,1,0:T(8,128)} %get-tuple-element.12), channel_id=1, source_target_pairs={{0,1},{1,2},{2,3},{3,4},{4,5},{5,6},{6,7},{8,9},{9,10},{10,11},{11... | collective-permute-start | bytes 2359304 | tf_op jit(solution)/shard_map/ppermute | solution.py:17
  29.0 268.2 %collective-permute-start.1 = (f32[1,768,256]{2,1,0:T(8,128)}, f32[1,768,256]{2,1,0:T(8,128)}, u32[]{:S(2)}, u32[]{:S(2)}) collective-permute-start(f32[1,768,256]{2,1,0:T(8,128)} %get-tuple-element.13), channel_id=1, source_target_pairs={{1,0},{2,1},{3,2},{4,3},{5,4},{6,5},{7,6},{9,8},{10,9},{11,10},{12... | collective-permute-start | bytes 2359304 | tf_op jit(solution)/shard_map/ppermute | solution.py:19
  30.3 1.2 copy-start.3
  43.7 4.0 copy-start.4
  297.1 1.4 copy-start.1
  297.1 311.4 %all-gather.7.cloned.1.call-start = ((), (), s32[]{:S(2)}) async-start(), calls=%async_computation.3 | async-start | bytes 18874368 | tf_op jit(solution)/shard_map/all_gather | solution.py:56
  364.6 337.1 %all-reduce.5.cloned.1.call-start = ((), (), s32[]{:S(2)}) async-start(), calls=%async_computation.1 | async-start | bytes 3145728 | tf_op jit(solution)/shard_map/psum | solution.py:67
  383.6 276.8 %collective-permute-start.2 = (f32[1,768,256]{2,1,0:T(8,128)}, f32[1,768,256]{2,1,0:T(8,128)}, u32[]{:S(2)}, u32[]{:S(2)}) collective-permute-start(f32[1,768,256]{2,1,0:T(8,128)} %get-tuple-element.10), channel_id=1, source_target_pairs={{0,1},{1,2},{2,3},{3,4},{4,5},{5,6},{6,7},{8,9},{9,10},{10,11},{11... | collective-permute-start | bytes 2359304 | tf_op jit(solution)/shard_map/ppermute | solution.py:17
  387.9 272.6 %collective-permute-start.3 = (f32[1,768,256]{2,1,0:T(8,128)}, f32[1,768,256]{2,1,0:T(8,128)}, u32[]{:S(2)}, u32[]{:S(2)}) collective-permute-start(f32[1,768,256]{2,1,0:T(8,128)} %get-tuple-element.11), channel_id=1, source_target_pairs={{1,0},{2,1},{3,2},{4,3},{5,4},{6,5},{7,6},{9,8},{10,9},{11,10},{12... | collective-permute-start | bytes 2359304 | tf_op jit(solution)/shard_map/ppermute | solution.py:19
  660.4 1.4 copy-start.2
Sparse Core Ops, SparseCore 0:
  20.6 243.2 all-gather.4
  297.3 41.0 all-reduce.2
  364.7 243.7 all-gather.6
  660.6 41.0 all-reduce.4
